TPU v7x, 256 devices: a whole 4x4x8 slice. The times are simulated.
256 devices in a mesh: row: 4 (over z_lo, core), col: 64 (over y, x, z_hi).
Axes of the slice: x: 4, y: 4, z: 8 (z_hi: 4, z_lo: 2; z = z_hi * 2 + z_lo), core: 2. Of those that a mesh axis runs over, the one named last changes fastest.
Arguments:
- matrix_t: bfloat16 [30720, 30720], P('col', 'row')
- fibers: float32 [3, 131072], P(None, 'col'), may hold values from -0.7 to 0.7, as said below
- forces: float32 [3, 131072], P(None, 'col'), may hold values from -0.375 to 0.375
- nodes: float32 [3, 10240], P(None, 'row'), may hold values from -1 to 1, as said below
- node_order: int32 [10240], replicated, may hold values from 0 to 10239, each once
Outputs:
- velocity: float32 [30720], P(('row', 'col'))
- density: float32 [30720], P(('row', 'col'))
Inputs may be any that keep to these rules, and one draw needn't show every extreme that they name: node_order holds every number below 10240 once. `nodes`: every node lies on the unit sphere about the anchor. `fibers`: every fiber point lies within distance 0.7 of the anchor.
All inputs are finite; a program needn't handle non-finite values.
Results may differ from a plain program's by a relative error of at most 0.00067.
Values may be sent and summed in bfloat16 or wider, within the bound.
A program may use at most 64 MiB of HBM per device.

v0:
```python
import math
import jax
import jax.numpy as jnp
from jax import lax
from jax.sharding import PartitionSpec as P

inv_eight_pi = 1.0 / (8.0 * math.pi)
tiny_eps = 1e-06


def stokeslet_sum(targets, sources, strengths):
    count_src = sources.shape[1]
    width_blk = math.gcd(count_src, 256)

    def advance(turn_index, running):
        source = lax.dynamic_slice_in_dim(sources, turn_index * width_blk, width_blk, 1)
        force_block = lax.dynamic_slice_in_dim(strengths, turn_index * width_blk, width_blk, 1)
        offset = targets[:, None, :] - source[:, :, None]
        inverse = 1.0 / jnp.sqrt(jnp.sum(offset * offset, axis=0))
        projected = jnp.sum(offset * force_block[:, :, None], axis=0) * (
            inverse * inverse * inverse
        )
        return running + jnp.sum(
            force_block[:, :, None] * inverse[None] + offset * projected[None], axis=1
        )

    running = lax.fori_loop(
        0, count_src // width_blk, advance, jnp.zeros(targets.shape, jnp.float32)
    )
    return running * inv_eight_pi


def givens_solve(initial_norm, entry_11, entry_21, entry_12, entry_22, entry_32):
    radius_one = jnp.sqrt(entry_11 * entry_11 + entry_21 * entry_21)
    cosine_one = entry_11 / radius_one
    sine_one = entry_21 / radius_one
    upper_12 = cosine_one * entry_12 + sine_one * entry_22
    lower_22 = cosine_one * entry_22 - sine_one * entry_12
    radius_two = jnp.sqrt(lower_22 * lower_22 + entry_32 * entry_32)
    weight_two = lower_22 / radius_two * (-sine_one * initial_norm) / radius_two
    weight_one = (cosine_one * initial_norm - upper_12 * weight_two) / radius_one
    return (weight_one, weight_two)


def shards(matrix_t, fibers, forces, nodes, node_order):
    width_cols = matrix_t.shape[0]
    block_rows = matrix_t.shape[1]
    piece_rows = block_rows // lax.axis_size("col")
    row_place = lax.axis_index("row")
    col_place = lax.axis_index("col")
    all_nodes = lax.all_gather(nodes, "row", axis=1, tiled=True)
    node_count = block_rows // 3
    my_order = lax.dynamic_slice_in_dim(node_order, row_place * node_count, node_count)
    targets = jnp.take(all_nodes, my_order, axis=1)

    def gather_whole(rounded):
        return lax.all_gather(rounded, "row", axis=0, tiled=True)

    def column_operand(vector):
        rounded = vector.astype(jnp.bfloat16)
        whole = gather_whole(rounded)
        return lax.dynamic_slice_in_dim(whole, col_place * width_cols, width_cols)

    def sum_dots(stacked):
        return lax.psum(stacked, "row")

    def apply_operator(vector):
        column_part = column_operand(vector)
        product = jnp.dot(column_part, matrix_t, preferred_element_type=jnp.float32)
        return lax.psum(product, "col") + vector

    def to_piece(vector):
        return lax.dynamic_slice_in_dim(vector, col_place * piece_rows, piece_rows)

    velocity = lax.psum(stokeslet_sum(targets, fibers, forces).T.reshape(-1), "col")
    initial_norm = jnp.sqrt(sum_dots(jnp.stack([jnp.sum(velocity * velocity)]))[0] + tiny_eps)
    basis_one = velocity / initial_norm
    image_one = apply_operator(basis_one)
    entry_11 = sum_dots(jnp.stack([jnp.sum(basis_one * image_one)]))[0]
    rest_one = image_one - entry_11 * basis_one
    entry_21 = jnp.sqrt(sum_dots(jnp.stack([jnp.sum(rest_one * rest_one)]))[0] + tiny_eps)
    basis_two = rest_one / entry_21
    image_two = apply_operator(basis_two)
    entry_12 = sum_dots(jnp.stack([jnp.sum(basis_one * image_two)]))[0]
    partial_two = image_two - entry_12 * basis_one
    entry_22 = sum_dots(jnp.stack([jnp.sum(basis_two * partial_two)]))[0]
    rest_two = partial_two - entry_22 * basis_two
    entry_32 = jnp.sqrt(sum_dots(jnp.stack([jnp.sum(rest_two * rest_two)]))[0] + tiny_eps)
    weight_one, weight_two = givens_solve(
        initial_norm, entry_11, entry_21, entry_12, entry_22, entry_32
    )
    density = weight_one * basis_one + weight_two * basis_two
    return (to_piece(velocity), to_piece(density))


def solution(mesh):
    return jax.shard_map(
        shards,
        mesh=mesh,
        in_specs=(P("col", "row"), P(None, "col"), P(None, "col"), P(None, "row"), P()),
        out_specs=(P(("row", "col")), P(("row", "col"))),
        check_vma=False,
    )
```

profile of v0, /device:TPU:1, one launch (start us, length us, event | category | flops | bytes accessed | tf_op | source)
XLA Modules:
  0.0 1287.9 jit_solution(4615934349465660564)
XLA Ops:
  0.6 0.8 compare_and_fusion
  1.4 1.2 copy.15
  2.7 35.1 %all_gather.9 = f32[3,10240]{0,1:T(8,128)} all-gather(f32[3,2560]{0,1:T(8,128)S(1)} %copy.15), channel_id=1, replica_groups=mesh['row'=4,'col'=64] {'row'}, dimensions={1}, use_global_device_ids=true | all-gather | bytes 153600 | tf_op jit(solution)/shard_map/all_gather | solution.py:51
  37.7 6.6 gather_fusion
  44.4 1.4 select_bitcast_fusion
  46.1 46.0 %while.14 = (s32[]{:T(128)}, f32[3,2560]{1,0:T(4,128)S(1)}, f32[3,2048]{1,0:T(4,128)}, f32[3,2560]{1,0:T(4,128)S(1)}, f32[3,2048]{1,0:T(4,128)}, /*index=5*/s32[]{:T(128)}, s32[]{:T(128)}, s32[]{:T(128)}, s32[]{:T(128)}) while((s32[]{:T(128)}, f32[3,2560]{1,0:T(4,128)S(1)}, f32[3,2048]{1,0:T(4,128)}, f32[3,2560]{1,0:T(4,128)S(1)}, ...), condition=%wide.region_4.5_spmd.clone, body=%wide.region_0.4_spmd.clone.sunk | while | flops 20323844 | bytes 21180568 | solution.py:27
  46.1 0.7 constant_dynamic-slice_fusion.3
  46.9 2.1 fusion.16
  49.0 0.7 fusion.17
  49.7 2.1 fusion.18
  52.6 2.1 fusion.16
  54.7 0.7 fusion.17
  55.5 2.1 fusion.18
  58.4 2.1 fusion.16
  60.5 0.7 fusion.17
  61.2 2.1 fusion.18
  64.1 2.1 fusion.16
  66.2 0.7 fusion.17
  67.0 2.1 fusion.18
  69.9 2.1 fusion.16
  72.0 0.7 fusion.17
  72.7 2.1 fusion.18
  75.6 2.1 fusion.16
  77.7 0.7 fusion.17
  78.5 2.1 fusion.18
  81.4 2.1 fusion.16
  83.5 0.7 fusion.17
  84.2 2.1 fusion.18
  87.1 2.1 fusion.16
  89.2 0.7 fusion.17
  90.0 2.1 fusion.18
  92.6 0.9 reshape.41
  93.5 325.3 %psum.63 = f32[7680]{0:T(1024)S(1)} all-reduce(f32[7680]{0:T(1024)S(1)} %reshape.41), channel_id=1, replica_groups=mesh['row'=4,'col'=64] {'col'}, use_global_device_ids=true, to_apply=%region_5.6 | all-reduce | flops 7680 | bytes 61440 | tf_op jit(solution)/shard_map/psum | solution.py:75
  419.4 60.8 %psum.64 = f32[1]{0:T(128)} all-reduce(f32[1]{0:T(128)} %bitcast.2), channel_id=1, replica_groups=mesh['row'=4,'col'=64] {'row'}, use_global_device_ids=true, to_apply=%region_7.8 | all-reduce | flops 1 | bytes 8 | tf_op jit(solution)/shard_map/psum | solution.py:65
  480.9 5.9 all-gather
  487.3 4.2 convolution_reduce_fusion.1
  491.4 315.2 %psum.65 = f32[7680]{0:T(1024)S(1)} all-reduce(f32[7680]{0:T(1024)S(1)} %convolution_reduce_fusion.1), channel_id=1, replica_groups=mesh['row'=4,'col'=64] {'col'}, use_global_device_ids=true, to_apply=%region_8.9 | all-reduce | flops 7680 | bytes 61440 | tf_op jit(solution)/shard_map/psum | solution.py:70
  807.3 60.8 %psum.66 = f32[]{:T(128)} all-reduce(f32[]{:T(128)} %get-tuple-element.151), channel_id=1, replica_groups=mesh['row'=4,'col'=64] {'row'}, use_global_device_ids=true, to_apply=%region_10.11 | all-reduce | flops 1 | bytes 8 | tf_op jit(solution)/shard_map/psum | solution.py:65
  868.0 1.3 multiply_reduce_fusion.3
  869.4 6.3 psum.67
  878.3 6.6 all-gather.1
  885.4 4.2 convolution_reduce_fusion
  889.6 315.2 %psum.68 = f32[7680]{0:T(1024)S(1)} all-reduce(f32[7680]{0:T(1024)S(1)} %convolution_reduce_fusion), channel_id=1, replica_groups=mesh['row'=4,'col'=64] {'col'}, use_global_device_ids=true, to_apply=%region_13.14 | all-reduce | flops 7680 | bytes 61440 | tf_op jit(solution)/shard_map/psum | solution.py:70
  1205.4 60.9 %psum.69 = f32[]{:T(128)} all-reduce(f32[]{:T(128)} %get-tuple-element.147), channel_id=1, replica_groups=mesh['row'=4,'col'=64] {'row'}, use_global_device_ids=true, to_apply=%region_15.16 | all-reduce | flops 1 | bytes 8 | tf_op jit(solution)/shard_map/psum | solution.py:65
  1266.3 1.3 multiply_reduce_fusion.1
  1267.6 6.3 psum.70
  1275.7 1.9 multiply_reduce_fusion
  1277.6 7.0 psum.71
  (37 shorter events, 10.8 us)
where the time goes:
time: 1290 us
  blocking collectives  1210 us (94%)
  other arithmetic  50.4 us (4%)
  local copies, waits for them, and re-layouts  16.1 us (1%)
    psum x2, blocking collectives, apply_operator(): return lax.psum(product, 'col') + vector  630 us
    psum x1, blocking collectives, shards(): lax.psum(stokeslet_sum(targets, fibers, forces).T.reshape(-1), 'col')  325 us
    psum x6, blocking collectives, sum_dots(): return lax.psum(stacked, 'row')  202 us
    all_gather x1, blocking collectives, shards(): all_nodes = lax.all_gather(nodes, 'row', axis=1, tiled=True)  35.1 us

commit v1 on v0

--- a/solution.py
+++ b/solution.py
@@ -72,7 +72,9 @@
     def to_piece(vector):
         return lax.dynamic_slice_in_dim(vector, col_place * piece_rows, piece_rows)
 
-    velocity = lax.psum(stokeslet_sum(targets, fibers, forces).T.reshape(-1), "col")
+    velocity = jnp.sum(
+        lax.all_gather(stokeslet_sum(targets, fibers, forces).T.reshape(-1), "col"), axis=0
+    )
     initial_norm = jnp.sqrt(sum_dots(jnp.stack([jnp.sum(velocity * velocity)]))[0] + tiny_eps)
     basis_one = velocity / initial_norm
     image_one = apply_operator(basis_one)

time: 1290 us -> 1010 us (0.78)
  blocking collectives: 1210 us -> 833 us
  waiting for transfers between devices: 0 us -> 77.8 us
  between operations: 7.48 us -> 21.1 us
    psum x1 -> x0, blocking collectives: 325 us -> none  [shards(): lax.psum(stokeslet_sum(targets, fibers, forces).T.reshape(-1), 'col')]
    all_gather x0 -> x1, waiting for transfers between devices: none -> 77.7 us  [shards(): lax.all_gather(stokeslet_sum(targets, fibers, forces).T.reshape(-1), 'col')]
    psum x6, blocking collectives: 202 us -> 150 us  [sum_dots(): return lax.psum(stacked, 'row')]
  transfers between devices with their start and end apart: 0 -> 1, of which waited for: 0 -> 1; matrix products, arithmetic and copies ran while one was open for 0% -> 0% of each run, Pallas kernels for 0% -> 0%
where the time goes in v1:
time: 1010 us
  blocking collectives  833 us (82%)
  waiting for transfers between devices  77.8 us (8%)
  other arithmetic  53.2 us (5%)
  between operations  21.1 us (2%)
  local copies, waits for them, and re-layouts  16.7 us (2%)
    psum x2, blocking collectives, apply_operator(): return lax.psum(product, 'col') + vector  636 us
    psum x6, blocking collectives, sum_dots(): return lax.psum(stacked, 'row')  150 us
    all_gather x1, waiting for transfers between devices, shards(): lax.all_gather(stokeslet_sum(targets, fibers, forces).T.reshape(-1), 'col')  77.7 us
    all_gather x1, blocking collectives, shards(): all_nodes = lax.all_gather(nodes, 'row', axis=1, tiled=True)  35.1 us
  transfers between devices with their start and end apart: 1, of which 1 were waited for; matrix products, arithmetic and copies ran while one was open for 0% of the time, Pallas kernels for 0%

profile of v1, /device:TPU:1, one launch (start us, length us, event | category | flops | bytes accessed | tf_op | source)
XLA Modules:
  0.0 1010.6 jit_solution(4598976422078961401)
XLA Ops:
  7.2 0.8 compare_and_fusion
  8.0 1.2 copy.15
  9.3 35.1 %all_gather.12 = f32[3,10240]{0,1:T(8,128)} all-gather(f32[3,2560]{0,1:T(8,128)S(1)} %copy.15), channel_id=1, replica_groups=mesh['row'=4,'col'=64] {'row'}, dimensions={1}, use_global_device_ids=true | all-gather | bytes 153600 | tf_op jit(solution)/shard_map/all_gather | solution.py:51
  44.3 6.6 gather_fusion
  51.0 1.4 select_bitcast_fusion
  52.7 46.0 %while.14 = (s32[]{:T(128)}, f32[3,2560]{1,0:T(4,128)S(1)}, f32[3,2048]{1,0:T(4,128)}, f32[3,2560]{1,0:T(4,128)S(1)}, f32[3,2048]{1,0:T(4,128)}, /*index=5*/s32[]{:T(128)}, s32[]{:T(128)}, s32[]{:T(128)}, s32[]{:T(128)}) while((s32[]{:T(128)}, f32[3,2560]{1,0:T(4,128)S(1)}, f32[3,2048]{1,0:T(4,128)}, f32[3,2560]{1,0:T(4,128)S(1)}, ...), condition=%wide.region_4.5_spmd.clone, body=%wide.region_0.4_spmd.clone.sunk | while | flops 20323844 | bytes 21180568 | solution.py:27
  53.5 2.1 fusion.16
  55.6 0.7 fusion.17
  56.3 2.1 fusion.18
  59.2 2.1 fusion.16
  61.3 0.7 fusion.17
  62.1 2.1 fusion.18
  65.0 2.1 fusion.16
  67.1 0.7 fusion.17
  67.8 2.1 fusion.18
  70.7 2.1 fusion.16
  72.8 0.7 fusion.17
  73.6 2.1 fusion.18
  76.5 2.1 fusion.16
  78.6 0.7 fusion.17
  79.3 2.1 fusion.18
  82.2 2.1 fusion.16
  84.3 0.7 fusion.17
  85.1 2.1 fusion.18
  88.0 2.1 fusion.16
  90.1 0.7 fusion.17
  90.8 2.1 fusion.18
  93.7 2.1 fusion.16
  95.8 0.7 fusion.17
  96.6 2.1 fusion.18
  99.2 1.5 reshape.50
  100.7 77.7 %all-gather.5.cloned.1.call-done = f32[64,1,7680]{2,1,0:T(1,128)} async-done(((f32[1,1,7680]{2,1,0:T(1,128)}), f32[64,1,7680]{2,1,0:T(1,128)}) %all-gather.5.cloned.1.call-update) | async-done | bytes 1966096 | tf_op jit(solution)/shard_map/all_gather | solution.py:76
  178.5 2.7 reduce_sum.102
  181.8 7.9 psum.56
  190.4 6.2 all-gather.1
  197.1 4.2 convolution_reduce_fusion.1
  201.2 321.0 %psum.57 = f32[7680]{0:T(1024)S(1)} all-reduce(f32[7680]{0:T(1024)S(1)} %convolution_reduce_fusion.1), channel_id=1, replica_groups=mesh['row'=4,'col'=64] {'col'}, use_global_device_ids=true, to_apply=%region_8.9 | all-reduce | flops 7680 | bytes 61440 | tf_op jit(solution)/shard_map/psum | solution.py:70
  522.8 61.2 %psum.58 = f32[]{:T(128)} all-reduce(f32[]{:T(128)} %get-tuple-element.151), channel_id=1, replica_groups=mesh['row'=4,'col'=64] {'row'}, use_global_device_ids=true, to_apply=%region_10.11 | all-reduce | flops 1 | bytes 8 | tf_op jit(solution)/shard_map/psum | solution.py:65
  585.3 1.3 multiply_reduce_fusion.3
  586.6 6.4 psum.59
  594.4 6.0 all-gather.2
  600.8 4.2 convolution_reduce_fusion
  605.0 315.1 %psum.60 = f32[7680]{0:T(1024)S(1)} all-reduce(f32[7680]{0:T(1024)S(1)} %convolution_reduce_fusion), channel_id=1, replica_groups=mesh['row'=4,'col'=64] {'col'}, use_global_device_ids=true, to_apply=%region_13.14 | all-reduce | flops 7680 | bytes 61440 | tf_op jit(solution)/shard_map/psum | solution.py:70
  920.7 60.9 %psum.61 = f32[]{:T(128)} all-reduce(f32[]{:T(128)} %get-tuple-element.147), channel_id=1, replica_groups=mesh['row'=4,'col'=64] {'row'}, use_global_device_ids=true, to_apply=%region_15.16 | all-reduce | flops 1 | bytes 8 | tf_op jit(solution)/shard_map/psum | solution.py:65
  981.7 1.3 multiply_reduce_fusion.1
  983.6 6.2 psum.62
  990.5 1.9 multiply_reduce_fusion
  994.4 7.2 psum.63
  (40 shorter events, 11.6 us)
Async XLA Ops:
  7.2 171.3 %all-gather.5.cloned.1.call-start = ((), (), s32[]{:S(2)}) async-start(), calls=%async_computation | async-start | bytes 1996800 | tf_op jit(solution)/shard_map/all_gather | solution.py:76
Sparse Core Ops, SparseCore 0:
  100.8 77.5 all-gather.4
